TPU v7x, 256 devices: a whole 4x4x8 slice. The times are simulated.
256 devices in a mesh: section: 8 (over z_hi, x), seq: 32 (over y, z_lo, core).
Axes of the slice: x: 4, y: 4, z: 8 (z_hi: 2, z_lo: 4; z = z_hi * 4 + z_lo), core: 2. Of those that a mesh axis runs over, the one named last changes fastest.
Arguments:
- input_keys: bfloat16 [8, 16384, 2048], P('section', 'seq'), may hold values from -6 to 6
- input_values: bfloat16 [8, 16384, 2048], P('section', 'seq'), may hold values from -6 to 6
- latent_queries: bfloat16 [8, 1024, 2048], P('section', 'seq'), may hold values from -6 to 6
- forward_out: bfloat16 [8, 1024, 2048], P('section', 'seq'), may hold values from -0.59765625 to 0.59765625
- log_norms: float32 [8, 1024, 16], P('section'), as said below
- block_table: int32 [8, 8], P('section'), may hold values from 0 to 127, as said below
- layer_grads: float32 [8, 8, 1024, 2048], P('section', None, 'seq'), may hold values from -600 to 600
Outputs:
- grad_keys: bfloat16 [8, 16384, 2048], P('section', 'seq')
- grad_values: bfloat16 [8, 16384, 2048], P('section', 'seq')
- grad_queries: bfloat16 [8, 1024, 2048], P('section', 'seq')
Inputs may be any that keep to these rules, and one draw needn't show every extreme that they name: block_table[b, a] is the last block of 128 input positions that latent block a sees; it rises strictly with a, it lies from 16 * (a + 1) - 8 to 16 * (a + 1) - 1, and the last latent block sees every position. log_norms[b, i, h] stand in for the saved normalizers: they are drawn near the log of the number of positions that latent i sees, plus 0.5, with noise of at most 0.45 either way.
All inputs are finite; a program needn't handle non-finite values.
Results may differ from a plain program's by a relative error of at most 0.0058.
Values may be sent and summed in bfloat16 or wider, within the bound.
No kernel may reach another device: no remote copies, remote signals or barrier semaphores. Data moves between devices by JAX's collectives and lax.ppermute only.
A program may use at most 128 MiB of HBM per device.

v0:
```python
import math

import jax
import jax.numpy as jnp
from jax import lax
from jax.sharding import PartitionSpec as P

BLK = 128


def body(
    input_keys, input_values, latent_queries, forward_out, log_norms, block_table, layer_grads
):
    arrived = lax.psum_scatter(layer_grads, "section", scatter_dimension=1, tiled=True)
    out_grad = arrived[0, 0].astype(jnp.bfloat16)
    head_count = log_norms.shape[2]
    width = input_keys.shape[2]
    head_dim = width // head_count
    score_scale = 1.0 / math.sqrt(head_dim)
    tok_count = input_keys.shape[1]
    limits = jnp.repeat(block_table[0], BLK)
    unit = lax.axis_index("seq")
    key_block = (unit * tok_count + jnp.arange(tok_count)) // BLK
    key_heads = input_keys[0].reshape(tok_count, head_count, head_dim).transpose(1, 0, 2)
    val_heads = input_values[0].reshape(tok_count, head_count, head_dim).transpose(1, 0, 2)
    lat_stack = jnp.stack([latent_queries[0], out_grad, forward_out[0]])
    all_lse = log_norms[0]
    lat_total = all_lse.shape[0]
    zeros_tok = jnp.zeros((head_count, tok_count, head_dim), jnp.float32)
    zeros_lat = jnp.zeros((lat_total, head_count, head_dim), jnp.float32)
    totals = (zeros_tok, zeros_tok, zeros_lat)
    latent_piece = lax.all_gather(lat_stack, "seq", axis=1, tiled=True)
    row_count = latent_piece.shape[1]
    step_rows = math.gcd(row_count, 256)
    step_count = row_count // step_rows
    split = latent_piece.reshape(3, step_count, step_rows, head_count, head_dim).transpose(
        1, 0, 2, 3, 4
    )

    def row_step(carry, inputs):
        key_total, value_total, query_total = carry
        lat_block, step_index = inputs
        row_start = step_index * step_rows
        queries = lat_block[0]
        grads = lat_block[1]
        lse_rows = lax.dynamic_slice_in_dim(all_lse, row_start, step_rows, 0)
        lim_rows = lax.dynamic_slice_in_dim(limits, row_start, step_rows, 0)
        visible = key_block[None, :] <= lim_rows[:, None]
        delta = jnp.sum(grads.astype(jnp.float32) * lat_block[2].astype(jnp.float32), axis=2)
        scores = (
            jnp.einsum("ihc,hjc->hij", queries, key_heads, preferred_element_type=jnp.float32)
            * score_scale
        )
        probs = jnp.where(visible[None], jnp.exp(scores - lse_rows.T[:, :, None]), 0.0)
        probs_low = probs.astype(jnp.bfloat16)
        dprobs = jnp.einsum("ihc,hjc->hij", grads, val_heads, preferred_element_type=jnp.float32)
        dscores = (probs * (dprobs - delta.T[:, :, None])).astype(jnp.bfloat16)
        query_part = jnp.einsum(
            "hij,hjc->ihc", dscores, key_heads, preferred_element_type=jnp.float32
        )
        key_total = key_total + jnp.einsum(
            "hij,ihc->hjc", dscores, queries, preferred_element_type=jnp.float32
        )
        value_total = value_total + jnp.einsum(
            "hij,ihc->hjc", probs_low, grads, preferred_element_type=jnp.float32
        )
        old_rows = lax.dynamic_slice_in_dim(query_total, row_start, step_rows, 0)
        query_total = lax.dynamic_update_slice_in_dim(
            query_total, old_rows + query_part, row_start, 0
        )
        return ((key_total, value_total, query_total), None)

    totals, ignored = lax.scan(row_step, totals, (split, jnp.arange(step_count, dtype=jnp.int32)))
    key_total, value_total, query_total = totals
    grad_k = (
        (key_total * score_scale).astype(jnp.bfloat16).transpose(1, 0, 2).reshape(tok_count, width)
    )
    grad_v = value_total.astype(jnp.bfloat16).transpose(1, 0, 2).reshape(tok_count, width)
    query_rows = lax.psum_scatter(
        query_total.reshape(lat_total, width) * score_scale, "seq", scatter_dimension=0, tiled=True
    )
    grad_q = query_rows.astype(jnp.bfloat16)
    return (grad_k[None], grad_v[None], grad_q[None])


def solution(mesh):
    placed = (
        P("section", "seq", None),
        P("section", "seq", None),
        P("section", "seq", None),
        P("section", "seq", None),
        P("section", None, None),
        P("section", None),
        P("section", None, "seq", None),
    )
    return jax.shard_map(
        body,
        mesh=mesh,
        in_specs=placed,
        out_specs=(P("section", "seq", None), P("section", "seq", None), P("section", "seq", None)),
        check_vma=False,
    )
```

profile of v0, /device:TPU:2, one launch (start us, length us, event | category | flops | bytes accessed | tf_op | source)
XLA Modules:
  0.0 489.3 jit_solution(8766786200359334464)
XLA Ops:
  7.2 0.7 reduce-scatter.3.cloned.1.call-update
  8.0 102.2 %reduce-scatter.3.cloned.1.call-done = f32[1,1,32,2048]{3,2,1,0:T(8,128)} async-done(((f32[1,8,32,2048]{3,2,1,0:T(8,128)}), f32[1,1,32,2048]{3,2,1,0:T(8,128)}) %reduce-scatter.3.cloned.1.call-update) | async-done | bytes 262160 | tf_op jit(solution)/shard_map/reduce_scatter | solution.py:14
  110.2 1.0 convert_bitcast_fusion.2
  111.2 1.8 pad_maximum_fusion
  113.0 2.5 copy.17
  115.6 3.0 copy.20
  118.6 4.0 copy.18
  122.5 3.9 copy.21
  126.5 61.8 %all-gather.2.cloned.1.call-done = bf16[3,1024,2048]{2,1,0:T(8,128)(2,1)} async-done(((bf16[3,32,2048]{2,1,0:T(8,128)(2,1)}), bf16[3,1024,2048]{2,1,0:T(8,128)(2,1)}) %all-gather.2.cloned.1.call-update) | async-done | bytes 12582928 | tf_op jit(solution)/shard_map/all_gather | solution.py:32
  188.3 11.4 %copy.32 = bf16[384,8,16,128]{3,2,1,0:T(8,128)(2,1)} copy(bf16[384,8,16,128]{3,1,2,0:T(8,128)(2,1)} %bitcast.89) | data formatting | bytes 25165824
  199.8 4.1 broadcast_in_dim.30
  203.8 106.4 %while.15 = (s32[]{:T(128)}, f32[16,512,128]{2,1,0:T(8,128)}, f32[16,512,128]{2,1,0:T(8,128)}, f32[1024,16,128]{2,0,1:T(8,128)}, s32[4]{0:T(128)S(1)}, /*index=5...) while((s32[]{:T(128)}, f32[16,512,128]{2,1,0:T(8,128)}, ...), condition=%wide.region_3.4_spmd.clone, body=%wide.region_1.3_spmd.clone.sunk | while | flops 2712276992 | bytes 86482224 | solution.py:73
  203.8 0.6 dynamic_slice.30
  205.1 0.7 dynamic-slice_bitcast_fusion.2
  205.9 0.1 broadcast_compare_fusion.2
  206.0 2.4 constant_dynamic-slice_fusion.4
  208.4 0.8 fusion.41
  209.3 1.3 fusion.40
  210.5 0.3 copy-done.3
  210.8 3.8 multiply_convert_fusion.3
  214.6 5.0 %select_add_fusion.5 = f32[16,512,128]{2,1,0:T(8,128)} fusion(f32[16,512,128]{2,1,0:T(8,128)} %get-tuple-element.234, pred[]{:T(512)S(6)} %compare.5, f32[16,256,512]{2,1,0:T(8,128)S(1)} %fusion.40, f32[16,256]{1,0:T(8,128)S(1)} %dynamic-slice_bitcast_fusion.2, pred[256,512]{1,0:T(8,128)(4,1)S(1)} %broadcast_compare_fusion.2, ...), kind=kOutput, calls=%fused_computation.5.clone.1 | convolution fusion | flops 547356672 | bytes 17973248 | tf_op jit(solution)/shard_map/while/body/eval_jaxpr/hij,ihc->hjc/dot_general | solution.py:64
  219.7 3.7 select_add_fusion.4
  223.3 4.3 fusion.42
  227.7 0.6 dynamic_slice.30
  229.0 0.7 dynamic-slice_bitcast_fusion.2
  229.7 0.1 broadcast_compare_fusion.2
  229.8 2.4 constant_dynamic-slice_fusion.4
  232.2 0.8 fusion.41
  233.1 1.3 fusion.40
  234.3 0.3 copy-done.3
  234.7 3.8 multiply_convert_fusion.3
  238.5 6.6 %select_add_fusion.5 = f32[16,512,128]{2,1,0:T(8,128)} fusion(f32[16,512,128]{2,1,0:T(8,128)} %get-tuple-element.234, pred[]{:T(512)S(6)} %compare.5, f32[16,256,512]{2,1,0:T(8,128)S(1)} %fusion.40, f32[16,256]{1,0:T(8,128)S(1)} %dynamic-slice_bitcast_fusion.2, pred[256,512]{1,0:T(8,128)(4,1)S(1)} %broadcast_compare_fusion.2, ...), kind=kOutput, calls=%fused_computation.5.clone.1 | convolution fusion | flops 547356672 | bytes 17973248 | tf_op jit(solution)/shard_map/while/body/eval_jaxpr/hij,ihc->hjc/dot_general | solution.py:64
  245.0 5.8 %select_add_fusion.4 = f32[16,512,128]{2,1,0:T(8,128)} fusion(f32[16,512,128]{2,1,0:T(8,128)} %get-tuple-element.233, bf16[16,256,512]{2,1,0:T(8,128)(2,1)S(1)} %multiply_convert_fusion.3, pred[]{:T(512)S(6)} %compare.5, bf16[1,1,256,16,128]{4,3,2,0,1:T(8,128)(2,1)S(1)} %get-tuple-element.212), kind=kOutput, calls=%fused_computation.6.clone.1 | convolution fusion | flops 538968064 | bytes 13631489 | tf_op jit(solution)/shard_map/while/body/eval_jaxpr/hij,ihc->hjc/dot_general | solution.py:61
  250.9 4.3 fusion.42
  255.2 0.6 dynamic_slice.30
  256.5 0.7 dynamic-slice_bitcast_fusion.2
  257.2 0.1 broadcast_compare_fusion.2
  257.3 2.4 constant_dynamic-slice_fusion.4
  259.7 0.8 fusion.41
  260.6 1.3 fusion.40
  261.8 0.3 copy-done.3
  262.2 3.8 multiply_convert_fusion.3
  265.9 6.6 %select_add_fusion.5 = f32[16,512,128]{2,1,0:T(8,128)} fusion(f32[16,512,128]{2,1,0:T(8,128)} %get-tuple-element.234, pred[]{:T(512)S(6)} %compare.5, f32[16,256,512]{2,1,0:T(8,128)S(1)} %fusion.40, f32[16,256]{1,0:T(8,128)S(1)} %dynamic-slice_bitcast_fusion.2, pred[256,512]{1,0:T(8,128)(4,1)S(1)} %broadcast_compare_fusion.2, ...), kind=kOutput, calls=%fused_computation.5.clone.1 | convolution fusion | flops 547356672 | bytes 17973248 | tf_op jit(solution)/shard_map/while/body/eval_jaxpr/hij,ihc->hjc/dot_general | solution.py:64
  272.5 5.8 %select_add_fusion.4 = f32[16,512,128]{2,1,0:T(8,128)} fusion(f32[16,512,128]{2,1,0:T(8,128)} %get-tuple-element.233, bf16[16,256,512]{2,1,0:T(8,128)(2,1)S(1)} %multiply_convert_fusion.3, pred[]{:T(512)S(6)} %compare.5, bf16[1,1,256,16,128]{4,3,2,0,1:T(8,128)(2,1)S(1)} %get-tuple-element.212), kind=kOutput, calls=%fused_computation.6.clone.1 | convolution fusion | flops 538968064 | bytes 13631489 | tf_op jit(solution)/shard_map/while/body/eval_jaxpr/hij,ihc->hjc/dot_general | solution.py:61
  278.4 4.4 fusion.42
  282.8 0.6 dynamic_slice.30
  284.1 0.7 dynamic-slice_bitcast_fusion.2
  284.8 0.1 broadcast_compare_fusion.2
  284.9 2.4 constant_dynamic-slice_fusion.4
  287.3 0.8 fusion.41
  288.2 1.3 fusion.40
  289.4 0.3 copy-done.3
  289.8 3.8 multiply_convert_fusion.3
  293.6 6.6 %select_add_fusion.5 = f32[16,512,128]{2,1,0:T(8,128)} fusion(f32[16,512,128]{2,1,0:T(8,128)} %get-tuple-element.234, pred[]{:T(512)S(6)} %compare.5, f32[16,256,512]{2,1,0:T(8,128)S(1)} %fusion.40, f32[16,256]{1,0:T(8,128)S(1)} %dynamic-slice_bitcast_fusion.2, pred[256,512]{1,0:T(8,128)(4,1)S(1)} %broadcast_compare_fusion.2, ...), kind=kOutput, calls=%fused_computation.5.clone.1 | convolution fusion | flops 547356672 | bytes 17973248 | tf_op jit(solution)/shard_map/while/body/eval_jaxpr/hij,ihc->hjc/dot_general | solution.py:64
  300.1 5.8 %select_add_fusion.4 = f32[16,512,128]{2,1,0:T(8,128)} fusion(f32[16,512,128]{2,1,0:T(8,128)} %get-tuple-element.233, bf16[16,256,512]{2,1,0:T(8,128)(2,1)S(1)} %multiply_convert_fusion.3, pred[]{:T(512)S(6)} %compare.5, bf16[1,1,256,16,128]{4,3,2,0,1:T(8,128)(2,1)S(1)} %get-tuple-element.212), kind=kOutput, calls=%fused_computation.6.clone.1 | convolution fusion | flops 538968064 | bytes 13631489 | tf_op jit(solution)/shard_map/while/body/eval_jaxpr/hij,ihc->hjc/dot_general | solution.py:61
  306.0 4.3 fusion.42
  310.2 7.9 %copy_bitcast_fusion.7 = f32[1024,2048]{1,0:T(8,128)} fusion(f32[1024,16,128]{2,0,1:T(8,128)} %get-tuple-element.64), kind=kLoop, calls=%fused_computation.35 | loop fusion | flops 2097152 | bytes 16777216 | tf_op jit(solution)/shard_map/mul | solution.py:80
  318.1 5.9 %fusion.19 = (bf16[512,16,128]{2,0,1:T(8,128)(2,1)S(1)}, bf16[512,16,128]{2,0,1:T(8,128)(2,1)}) fusion(f32[16,512,128]{2,1,0:T(8,128)} %get-tuple-element.62, f32[16,512,128]{2,1,0:T(8,128)} %get-tuple-element.63), kind=kLoop, calls=%fused_computation.38 | loop fusion | flops 3145728 | bytes 12582912 | tf_op jit(solution)/shard_map/transpose | solution.py:76
  324.0 1.4 copy.22
  325.4 2.3 broadcast_in_dim_reshape.6
  327.7 3.0 copy.23
  330.6 2.3 broadcast_in_dim_reshape.7
  332.9 148.2 %reduce-scatter.5.cloned.1.call-done = f32[32,2048]{1,0:T(8,128)} async-done(((f32[1024,2048]{1,0:T(8,128)}), f32[32,2048]{1,0:T(8,128)}) %reduce-scatter.5.cloned.1.call-update) | async-done | bytes 262160 | tf_op jit(solution)/shard_map/reduce_scatter | solution.py:79
  481.2 1.6 convert_bitcast_fusion.1
  (27 shorter events, 0.6 us)
Async XLA Ops:
  7.2 119.3 %copy-start = (s32[1,8]{1,0:T(1,128)S(1)}, s32[1,8]{1,0:T(1,128)}, u32[]{:S(2)}) copy-start(s32[1,8]{1,0:T(1,128)} %param.14) | copy-start | bytes 100
  7.2 105.9 %copy-start.2 = (bf16[1,512,2048]{2,1,0:T(8,128)(2,1)S(1)}, bf16[1,512,2048]{2,1,0:T(8,128)(2,1)}, u32[]{:S(2)}) copy-start(bf16[1,512,2048]{2,1,0:T(8,128)(2,1)} %param.9) | copy-start | bytes 6291460
  7.2 103.0 %reduce-scatter.3.cloned.1.call-start = ((), (), s32[]{:S(2)}) async-start(), calls=%async_computation.2 | async-start | bytes 2359296 | tf_op jit(solution)/shard_map/reduce_scatter | solution.py:14
  7.9 180.4 %all-gather.2.cloned.1.call-start = ((), (), s32[]{:S(2)}) async-start(), calls=%async_computation.3 | async-start | bytes 12976128 | tf_op jit(solution)/shard_map/all_gather | solution.py:32
  113.0 368.2 %reduce-scatter.5.cloned.1.call-start = ((), (), s32[]{:S(2)}) async-start(), calls=%async_computation.4 | async-start | bytes 8650752 | tf_op jit(solution)/shard_map/reduce_scatter | solution.py:79
  209.2 1.6 copy-start.3
  233.1 1.6 copy-start.3
  260.6 1.6 copy-start.3
  288.2 1.6 copy-start.3
  327.7 155.1 %copy-start.1 = (s32[1,8]{1,0:T(1,128)S(1)}, s32[1,8]{1,0:T(1,128)}, u32[]{:S(2)}) copy-start(s32[1,8]{1,0:T(1,128)} %param.14) | copy-start | bytes 100
Sparse Core Ops, SparseCore 0:
  12.1 98.0 reduce-scatter.2
  113.1 75.1 all-gather.1
  318.3 162.8 reduce-scatter.4
where the time goes:
time: 490 us; the launch traced here: 489 us
  waiting for transfers between devices  313 us (64%)
  matrix products  83.4 us (17%)
  local copies, waits for them, and re-layouts  54.4 us (11%)
  other arithmetic  22 us (4%)
  between operations  13.8 us (3%)
    reduce_scatter x1, waiting for transfers between devices, body(): lax.psum_scatter(query_total.reshape(lat_total, width) * score_scale, 'se...  148 us
    reduce_scatter x1, waiting for transfers between devices, body(): lax.psum_scatter(layer_grads, 'section', scatter_dimension=1, tiled=True)  102 us
    all_gather x1, waiting for transfers between devices, body(): latent_piece = lax.all_gather(lat_stack, 'seq', axis=1, tiled=True)  61.8 us
    unnamed x11, local copies, waits for them, and re-layouts  24.8 us
    dot_general x4, matrix products, row_step(): jnp.einsum('hij,ihc->hjc', probs_low, grads, preferred_element_type=jnp.f...  24.8 us
    dot_general x4, matrix products, row_step(): jnp.einsum('hij,ihc->hjc', dscores, queries, preferred_element_type=jnp.f...  21.2 us
    dot_general x4, matrix products, row_step(): jnp.einsum('hij,hjc->ihc', dscores, key_heads, preferred_element_type=jnp...  17.3 us
    dot_general x4, matrix products, row_step(): jnp.einsum('ihc,hjc->hij', grads, val_heads, preferred_element_type=jnp.f...  15.1 us
  transfers between devices with their start and end apart: 3, of which 3 were waited for; matrix products, arithmetic and copies ran while one was open for 6% of the time, Pallas kernels for 0%

commit v1 on v0

v1 whole, which is shorter than its diff:
```python
import functools
import math

import jax
import jax.numpy as jnp
from jax import lax
from jax.experimental import pallas as pl
from jax.experimental.pallas import tpu as pltpu
from jax.sharding import Mesh, PartitionSpec as P

SECTION = ("zhi", "x")
SEQ = ("y", "zlo", "core")
BLK = 128
HD = 128
HALF = 1024
HEADS = 8
SCALE = 1.0 / math.sqrt(HD)
EXP_SCALE = SCALE * math.log2(math.e)
FAR = -1e30
BF = jnp.bfloat16
F32 = jnp.float32
NN = (((1,), (0,)), ((), ()))
NT = (((1,), (1,)), ((), ()))
TN = (((0,), (0,)), ((), ()))
NEXT = ((0, 1), (1, 2), (2, 3))


def dot(a, b, dims):
    return lax.dot_general(a, b, dims, preferred_element_type=F32)


def pieces(x):
    hi = lax.reduce_precision(x, 8, 7)
    mid = lax.reduce_precision(x - hi, 8, 7)
    return hi, mid, x - hi - mid


def grad_kernel(info, keep, recv, out, mine, other):
    grad = (keep[...] + recv[...].astype(F32)).astype(BF)
    prod = grad.astype(F32) * out[...].astype(F32)
    rows = grad.shape[0]
    col = lax.broadcasted_iota(jnp.int32, (rows, HD), 1)
    for side in range(2):
        extra = jnp.zeros((rows, HD), F32)
        for head in range(HEADS):
            at = (side * HEADS + head) * HD
            rest = -jnp.sum(prod[:, at : at + HD], axis=1, keepdims=True)
            for piece in range(3):
                part = rest.astype(BF).astype(F32)
                extra = jnp.where(col == piece * HEADS + head, part, extra)
                rest = rest - part
        block = jnp.concatenate([grad[:, side * HALF : (side + 1) * HALF], extra.astype(BF)], 1)

        @pl.when(info[0] == side)
        def _():
            mine[...] = block

        @pl.when(info[0] != side)
        def _():
            other[...] = block


def spread_kernel(rows, sends):
    for place in range(4):
        for side in range(2):
            sends[2 * place + side] = rows[:, side * HALF : (side + 1) * HALF]


def attn_kernel(info, *refs, shifts, first, last, tile, group):
    kv, refs = refs[:4], refs[4:]
    count = len(shifts)
    chunks, refs = [refs[4 * i : 4 * i + 4] for i in range(count)], refs[4 * count :]
    if not first:
        dk_in, dv_in = refs[:2]
        refs = refs[2:]
    outs, refs = refs[: (4 if last else 2)], refs[(4 if last else 2) :]
    dqs, refs = refs[:count], refs[count:]
    q_wide, g_wide = refs
    half = kv[0].shape[0]
    rows = chunks[0][0].shape[0]
    seen = info[1] + shifts[0] < 4

    def put(side, at, cols, dk, dv):
        whole = slice(side * half + at.start, side * half + at.stop)
        if not first:
            dk, dv = (dk_in[whole, cols], dv_in[whole, cols]) if dk is None else (
                dk_in[whole, cols] + dk, dv_in[whole, cols] + dv)
        elif dk is None:
            dk = dv = jnp.zeros((at.stop - at.start, HD), F32)
        if last:
            outs[side][at, cols] = (dk * SCALE).astype(BF)
            outs[2 + side][at, cols] = dv.astype(BF)
        else:
            outs[0][whole, cols] = dk
            outs[1][whole, cols] = dv

    @pl.when(seen)
    def _():
        for sub in range(group):
            cols = slice(sub * HD, (sub + 1) * HD)
            head = pl.program_id(0) * group + sub
            for i, (q, q_extra, g, g_extra) in enumerate(chunks):
                at = slice(i * rows, (i + 1) * rows)
                q_wide[sub, at, :HD] = q[:, cols]
                q_wide[sub, at, HD:] = q_extra[...]
                g_wide[sub, at, :HD] = g[:, cols]
                g_wide[sub, at, HD:] = g_extra[...]
            col = lax.broadcasted_iota(jnp.int32, (BLK, HD), 1)
            total_q = None
            for side in range(2):
                for t in range(half // tile):
                    at = slice(t * tile, (t + 1) * tile)
                    pick = []
                    for j in range(tile // BLK):
                        block = (side * half + at.start) // BLK + j
                        miss = jnp.where(col < 24, (col & 7) - head, (col - 24) - block)
                        pick.append(jnp.where(miss == 0, 1.0, 0.0).astype(BF))
                    pick = jnp.concatenate(pick, 0)
                    k = kv[side][at, cols]
                    v = kv[2 + side][at, cols]
                    scores = dot(jnp.concatenate([k, pick], 1), q_wide[sub], NT)
                    probs = jnp.exp2(scores * EXP_SCALE)
                    dprobs = dot(jnp.concatenate([v, pick], 1), g_wide[sub], NT)
                    dscores = (probs * dprobs).astype(BF)
                    dv = dot(probs.astype(BF), g_wide[sub, :, :HD], NN)
                    dk = dot(dscores, q_wide[sub, :, :HD], NN)
                    put(side, at, cols, dk, dv)
                    part = dot(k, dscores, TN)
                    total_q = part if total_q is None else total_q + part
            for i, dq in enumerate(dqs):
                dq[:, cols] = (total_q[:, i * rows : (i + 1) * rows].T * SCALE).astype(BF)

    @pl.when(jnp.logical_not(seen))
    def _():
        for sub in range(group):
            for side in range(2):
                put(side, slice(0, half), slice(sub * HD, (sub + 1) * HD), None, None)
        for dq in dqs:
            dq[...] = jnp.zeros_like(dq)


def attention(info, kv, chunks, sums, last, tile=512, group=2):
    half = kv[0].shape[0]
    rows = chunks[0][3].shape[0]
    wide = group * HD
    steps = HEADS // group
    own = pl.BlockSpec((half, wide), lambda h, info: (0, info[0] * steps + h))
    one = pl.BlockSpec((half, wide), lambda h, info: (0, h))
    both = pl.BlockSpec((2 * half, wide), lambda h, info: (0, h))
    lat = pl.BlockSpec((rows, wide), lambda h, info: (0, h))
    last_block = pl.BlockSpec((rows, HD), lambda h, info: (0, HEADS))
    in_specs, args = [own, one, own, one], list(kv)
    for shift, q, q_extra, g in chunks:
        in_specs += [
            pl.BlockSpec((rows, wide), lambda h, info, s=shift: ((info[1] + s) % 4, h)),
            pl.BlockSpec((rows, HD), lambda h, info, s=shift: ((info[1] + s) % 4, 0)),
            lat,
            last_block,
        ]
        args += [q, q_extra, g, g]
    aliases = {}
    if sums is not None:
        if not last:
            aliases = {1 + len(args): 0, 2 + len(args): 1}
        in_specs += [both, both]
        args += list(sums)
    shape = lambda r, t: jax.ShapeDtypeStruct((r, HALF), t)
    if last:
        out_specs, out_shape = [one] * 4, [shape(half, BF)] * 4
    else:
        out_specs, out_shape = [both] * 2, [shape(2 * half, F32)] * 2
    out_specs += [lat] * len(chunks)
    out_shape += [shape(rows, BF)] * len(chunks)
    work = len(chunks) * rows * 2 * half * HALF
    kernel = functools.partial(
        attn_kernel,
        shifts=[c[0] for c in chunks],
        first=sums is None,
        last=last,
        tile=tile,
        group=group,
    )
    return pl.pallas_call(
        kernel,
        grid_spec=pltpu.PrefetchScalarGridSpec(
            num_scalar_prefetch=1,
            grid=(steps,),
            in_specs=in_specs,
            out_specs=out_specs,
            scratch_shapes=[pltpu.VMEM((group, len(chunks) * rows, 2 * HD), BF)] * 2,
        ),
        out_shape=out_shape,
        input_output_aliases=aliases,
        compiler_params=pltpu.CompilerParams(
            dimension_semantics=("arbitrary",), vmem_limit_bytes=60 << 20
        ),
        cost_estimate=pl.CostEstimate(
            flops=20 * work, bytes_accessed=16 << 20, transcendentals=work // HD
        ),
        name="attention_backward_" + "_".join(str(c[0]) for c in chunks),
    )(info, *args)


def swap(x, axis):
    return lax.ppermute(x, axis, [(0, 1), (1, 0)])


def exchange(x, axis):
    return lax.all_to_all(x, axis, 0, 0, tiled=True)


def shifted(x, axis, shift):
    return lax.ppermute(x, axis, [((i + shift) % 4, i) for i in range(4)])


def back(pairs):
    return [(b, a) for a, b in pairs]


def body(keys, values, latent_queries, forward_out, log_norms, block_table, layer_grads):
    zhi, x = lax.axis_index("zhi"), lax.axis_index("x")
    y, zlo, core = lax.axis_index("y"), lax.axis_index("zlo"), lax.axis_index("core")
    keys, values, queries = keys[0], values[0], latent_queries[0]
    own_rows, width = queries.shape
    all_rows = log_norms.shape[1]
    y_rows = all_rows // 4
    info = jnp.stack([core, y]).astype(jnp.int32)

    def relative(a, axis):
        a = lax.dynamic_slice_in_dim(jnp.concatenate([a, a], axis), zlo, 4, axis)
        return jnp.where(core == 0, a, jnp.flip(a, axis + 1))

    def joined(mine, there):
        first = jnp.where(core == 0, mine, there)
        second = jnp.where(core == 0, there, mine)
        return jnp.concatenate([first, second], axis=1)[None]

    terms = layer_grads[0].reshape(2, 4, own_rows, width)
    term = lambda j: lax.dynamic_index_in_dim(terms, (x + j) % 4, 1, keepdims=False)
    sends = [term(j).astype(BF) for j in (1, 2, 3)]
    arrived = [shifted(send, "x", 3 - j) for j, send in enumerate(sends)]
    terms = term(0) + sum(a.astype(F32) for a in arrived)
    keep = lax.dynamic_index_in_dim(terms, zhi, 0, keepdims=False)
    sent = lax.dynamic_index_in_dim(terms, 1 - zhi, 0, keepdims=False).astype(BF)
    recv = swap(sent, "zhi")

    other = (1 - core) * HALF
    k_pair = swap(lax.dynamic_slice_in_dim(keys, other, HALF, 1), "core")
    v_pair = swap(lax.dynamic_slice_in_dim(values, other, HALF, 1), "core")

    q_send = pl.pallas_call(
        spread_kernel,
        out_shape=jax.ShapeDtypeStruct((8, own_rows, HALF), BF),
        cost_estimate=pl.CostEstimate(flops=0, bytes_accessed=10 << 16, transcendentals=0),
        name="spread",
    )(queries)
    q_chunk = exchange(q_send, ("zlo", "core")).reshape(4, 2, own_rows, HALF)
    q_chunk = relative(q_chunk, 0).reshape(1, y_rows, HALF)
    q_all = exchange(jnp.broadcast_to(q_chunk, (4, y_rows, HALF)), "y").reshape(all_rows, HALF)

    norms = lax.dynamic_slice_in_dim(log_norms[0], core * HEADS, HEADS, 1) * -math.sqrt(HD)
    limits = jnp.broadcast_to(block_table[0][:, None], (8, BLK)).reshape(all_rows, 1)
    block = (y * 4 + zlo) * 8 + jnp.bitwise_xor(jnp.arange(8), 4 * core)[None, :]
    unseen = jnp.where(block <= limits, 0.0, FAR).astype(F32)
    q_extra = jnp.concatenate(
        [*pieces(norms), unseen, jnp.zeros((all_rows, HD - 32), F32)], axis=1
    ).astype(BF)
    q_extra = relative(q_extra.reshape(4, 4, 2, own_rows, HD), 1).reshape(all_rows, HD)

    recv, k_pair, v_pair, q_extra = lax.optimization_barrier((recv, k_pair, v_pair, q_extra))

    piece = jax.ShapeDtypeStruct((own_rows, HALF + HD), BF)
    mine, other = pl.pallas_call(
        grad_kernel,
        grid_spec=pltpu.PrefetchScalarGridSpec(
            num_scalar_prefetch=1,
            grid=(1,),
            in_specs=[pl.BlockSpec((own_rows, width), lambda i, info: (0, 0))] * 3,
            out_specs=[pl.BlockSpec((own_rows, HALF + HD), lambda i, info: (0, 0))] * 2,
        ),
        out_shape=[piece, piece],
        cost_estimate=pl.CostEstimate(flops=1 << 18, bytes_accessed=1 << 20, transcendentals=0),
        name="out_grad",
    )(info, keep, recv, forward_out[0])
    piece = jnp.concatenate([mine, swap(other, "core")], 0)
    g0 = jnp.concatenate([piece] + [shifted(piece, "zlo", j) for j in (1, 2, 3)], 0)

    g1 = lax.ppermute(g0, "y", back(NEXT))
    g3 = lax.ppermute(g0, "y", [(3, 0)])
    kv = (keys, k_pair, values, v_pair)
    g2 = lax.ppermute(g1, "y", back(NEXT[:2]))
    *sums, dq1, dq3 = attention(
        info, kv, [(1, q_all, q_extra, g1), (3, q_all, q_extra, g3)], None, False
    )
    got1 = lax.ppermute(dq1, "y", NEXT)
    got3 = lax.ppermute(dq3, "y", [(0, 3)])
    *sums, dq2 = attention(info, kv, [(2, q_all, q_extra, g2)], sums, False)

    def sent_along_z(dq):
        dq = dq.reshape(4, 2 * own_rows, HALF)
        return [dq[0]] + [shifted(dq[j], "zlo", 4 - j) for j in (1, 2, 3)]

    def added(parts):
        return sum(p.astype(F32) for p in parts)

    dq2, got1, got3, g0 = lax.optimization_barrier((dq2, got1, got3, g0))
    far = sent_along_z(dq2)
    dk, dk_pair, dv, dv_pair, dq0 = attention(info, kv, [(0, q_all, q_extra, g0)], sums, True)
    far, dq0, dk_pair, dv_pair = lax.optimization_barrier((far, dq0, dk_pair, dv_pair))
    near = sent_along_z(added([dq0, got1, got3]).astype(BF))
    far = lax.ppermute(added(far).astype(BF), "y", [(0, 2), (1, 3)])
    there = [swap(dk_pair, "core"), swap(dv_pair, "core")]
    grad_k, grad_v = joined(dk, there[0]), joined(dv, there[1])
    near, far, grad_k, grad_v = lax.optimization_barrier((near, far, grad_k, grad_v))
    dq = added([*near, far]).astype(BF)
    grad_q = joined(dq[:own_rows], swap(dq[own_rows:], "core"))
    return grad_k, grad_v, grad_q


def solution(mesh):
    parts = Mesh(mesh.devices.reshape(2, 4, 4, 4, 2), SECTION + SEQ)
    rows = P(SECTION, SEQ, None)
    placed = (
        rows, rows, rows, rows, P(SECTION, None, None), P(SECTION, None),
        P(SECTION, None, SEQ, None),
    )
    return jax.shard_map(
        body, mesh=parts, in_specs=placed, out_specs=(rows, rows, rows), check_vma=False
    )
```

time: 490 us -> 156 us (0.32)
  waiting for transfers between devices: 313 us -> 40.9 us
  matrix products: 83.4 us -> 0 us
  starting transfers between devices: 0.12 us -> 44.1 us
  Pallas kernels: 0 us -> 43.6 us
  local copies, waits for them, and re-layouts: 54.4 us -> 14.5 us
  between operations: 13.8 us -> 1 us
  other arithmetic: 22 us -> 9.42 us
    reduce_scatter x2 -> x0, waiting for transfers between devices: 250 us -> none  [the longest x1 148 us: body(): lax.psum_scatter(query_total.reshape(lat_total, width) * score_scale, 'se...]
    dot_general x20 -> x0, matrix products: 83.4 us -> none  [the longest x4 24.8 us: row_step(): jnp.einsum('hij,ihc->hjc', probs_low, grads, preferred_element_type=jnp.f...]
    all_gather x1 -> x0, waiting for transfers between devices: 61.8 us -> none  [body(): latent_piece = lax.all_gather(lat_stack, 'seq', axis=1, tiled=True)]
    pallas_call x0 -> x5, Pallas kernels: none -> 43.6 us  [the longest x3 39.2 us: attention(): pl.pallas_call(kernel, grid_spec=pltpu.PrefetchScalarGridSpec(num_scalar_...]
    ppermute x0 -> x25, waiting for transfers between devices: none -> 40.9 us  [the longest x12 23.2 us: shifted(): return lax.ppermute(x, axis, [((i + shift) % 4, i) for i in range(4)])]
    ppermute x0 -> x25, starting transfers between devices: none -> 33.7 us  [the longest x12 15.6 us: shifted(): return lax.ppermute(x, axis, [((i + shift) % 4, i) for i in range(4)])]
    unnamed x11 -> x20, local copies, waits for them, and re-layouts: 24.8 us -> 3.39 us
    all_to_all x0 -> x2, starting transfers between devices: none -> 10.4 us  [exchange(): return lax.all_to_all(x, axis, 0, 0, tiled=True)]
  transfers between devices with their start and end apart: 3 -> 27, of which waited for: 3 -> 8; matrix products, arithmetic and copies ran while one was open for 6% -> 13% of each run, Pallas kernels for 0% -> 27%
where the time goes in v1:
time: 156 us; the launch traced here: 153 us
  starting transfers between devices  44.1 us (28%)
  Pallas kernels  43.6 us (28%)
  waiting for transfers between devices  40.9 us (26%)
  local copies, waits for them, and re-layouts  14.5 us (9%)
  other arithmetic  9.42 us (6%)
    pallas_call x3, Pallas kernels, attention(): pl.pallas_call(kernel, grid_spec=pltpu.PrefetchScalarGridSpec(num_scalar_...  39.2 us
    ppermute x12, waiting for transfers between devices, shifted(): return lax.ppermute(x, axis, [((i + shift) % 4, i) for i in range(4)])  23.2 us
    ppermute x12, starting transfers between devices, shifted(): return lax.ppermute(x, axis, [((i + shift) % 4, i) for i in range(4)])  15.6 us
    ppermute x1, waiting for transfers between devices, body(): g1 = lax.ppermute(g0, 'y', back(NEXT))  14 us
    all_to_all x2, starting transfers between devices, exchange(): return lax.all_to_all(x, axis, 0, 0, tiled=True)  10.4 us
    ppermute x7, starting transfers between devices, swap(): return lax.ppermute(x, axis, [(0, 1), (1, 0)])  6.04 us
    ppermute x1, starting transfers between devices, body(): far = lax.ppermute(added(far).astype(BF), 'y', [(0, 2), (1, 3)])  3.88 us
    broadcast_in_dim x3, other arithmetic, joined(): return jnp.concatenate([first, second], axis=1)[None]  3.68 us
  transfers between devices with their start and end apart: 27, of which 8 were waited for; matrix products, arithmetic and copies ran while one was open for 13% of the time, Pallas kernels for 27%

profile of v1, /device:TPU:2, one launch (start us, length us, event | category | flops | bytes accessed | tf_op | source)
XLA Modules:
  0.0 153.4 jit_solution(2883351157309485926)
XLA Ops:
  0.6 1.7 %spread.1 = bf16[8,32,1024]{2,1,0:T(8,128)(2,1)} custom-call(bf16[32,2048]{1,0:T(8,128)(2,1)} %bitcast.66), custom_call_target="tpu_custom_call" | custom-call | bytes 655360 | tf_op jit(solution)/shard_map/spread/pallas_call | solution.py:251
  2.4 5.9 %all-to-all-start = ((bf16[8,32,1024]{2,1,0:T(8,128)(2,1)}), bf16[8,32,1024]{2,1,0:T(8,128)(2,1)S(1)}, u32[]{:S(2)}, u32[]{:S(2)}) async-start(bf16[8,32,1024]{2,1,0:T(8,128)(2,1)} %spread.1), calls=%async_computation | async-start | bytes 1048576 | tf_op jit(solution)/shard_map/all_to_all | solution.py:209
  8.3 2.3 %fusion.1 = (bf16[2,32,2048]{2,1,0:T(8,128)(2,1)}, bf16[2,32,2048]{2,1,0:T(8,128)(2,1)}, bf16[2,32,2048]{2,1,0:T(8,128)(2,1)S(1)}) fusion(f32[2,4,32,2048]{3,2,1,0:T(8,128)} %bitcast.54, s32[]{:T(128)S(6)} %select_n.106, s32[]{:T(128)S(6)} %select_n.108, s32[]{:T(128)S(6)} %select_n.110), kind=kLoop, calls=%fused_computation.21 | loop fusion | bytes 1572876 | tf_op jit(solution)/shard_map/convert_element_type | solution.py:240
  10.5 1.5 collective-permute-start
  12.0 1.1 collective-permute-start.1
  13.1 2.2 %collective-permute-start.2 = (bf16[2,32,2048]{2,1,0:T(8,128)(2,1)S(1)}, bf16[2,32,2048]{2,1,0:T(8,128)(2,1)}, u32[]{:S(2)}, u32[]{:S(2)}) collective-permute-start(bf16[2,32,2048]{2,1,0:T(8,128)(2,1)S(1)} %get-tuple-element.81), channel_id=1, source_target_pairs={{32,0},{64,32},{96,64},{0,96},{33,1},{65,33},{97,65},{1,97},{34,2}... | collective-permute-start | bytes 786440 | tf_op jit(solution)/shard_map/ppermute | solution.py:213
  15.3 1.3 dynamic-slice_bitcast_fusion
  16.7 2.3 %dynamic-slice_bitcast_fusion.1 = bf16[512,1024]{1,0:T(8,128)(2,1)} fusion(bf16[1,512,2048]{2,1,0:T(8,128)(2,1)} %param.7, s32[]{:T(128)S(6)} %select_n.112), kind=kLoop, calls=%fused_computation.6 | loop fusion | bytes 2097156 | tf_op jit(solution)/shard_map/dynamic_slice | solution.py:248
  19.0 0.5 collective-permute-start.4
  19.5 0.5 broadcast.36
  20.0 0.6 reduce.3
  20.6 0.1 copy.36
  20.7 0.1 copy.37
  20.8 0.2 mul.31
  21.0 0.1 fusion.5
  21.1 0.2 copy.40
  21.3 0.2 copy.39
  21.4 0.2 copy.38
  21.6 0.1 select_convert_fusion
  21.8 0.6 concatenate.27
  22.4 0.1 fusion.4
  22.6 0.6 pad_add_fusion.info
  23.1 0.8 reverse_select_fusion.1
  23.9 3.1 %collective-permute-done.2 = bf16[2,32,2048]{2,1,0:T(8,128)(2,1)} collective-permute-done((bf16[2,32,2048]{2,1,0:T(8,128)(2,1)S(1)}, bf16[2,32,2048]{2,1,0:T(8,128)(2,1)}, u32[]{:S(2)}, u32[]{:S(2)}) %collective-permute-start.2) | collective-permute-done | bytes 262176 | tf_op jit(solution)/shard_map/ppermute | solution.py:213
  27.0 1.4 bitcast_add_fusion
  28.4 4.8 %collective-permute-start.3 = (bf16[32,2048]{1,0:T(8,128)(2,1)S(1)}, bf16[32,2048]{1,0:T(8,128)(2,1)S(1)}, u32[]{:S(2)}, u32[]{:S(2)}) collective-permute-start(bf16[32,2048]{1,0:T(8,128)(2,1)S(1)} %fusion.6), channel_id=1, source_target_pairs={{0,128},{128,0},{1,129},{129,1},{2,130},{130,2},{3,131},{131,3},{4... | collective-permute-start | bytes 393224 | tf_op jit(solution)/shard_map/ppermute | solution.py:205
  33.2 0.7 dynamic-slice_bitcast_fusion.2.keep
  33.9 0.2 fusion
  34.1 0.1 reverse_select_fusion
  34.3 1.6 %broadcast_in_dim.44 = bf16[4,256,1024]{2,1,0:T(8,128)(2,1)} broadcast(bf16[256,1024]{1,0:T(8,128)(2,1)S(1)} %bitcast.48), dimensions={1,2} | broadcast | bytes 2621440 | tf_op jit(solution)/shard_map/broadcast_in_dim | solution.py:259
  35.9 4.5 %all-to-all-start.1 = ((bf16[4,256,1024]{2,1,0:T(8,128)(2,1)}), bf16[4,256,1024]{2,1,0:T(8,128)(2,1)S(1)}, u32[]{:S(2)}, u32[]{:S(2)}) async-start(bf16[4,256,1024]{2,1,0:T(8,128)(2,1)} %broadcast_in_dim.44), calls=%async_computation.1 | async-start | bytes 4194304 | tf_op jit(solution)/shard_map/all_to_all | solution.py:209
  40.4 0.6 copy-done.3
  41.0 2.6 %out_grad.1 = (bf16[32,1152]{1,0:T(8,128)(2,1)}, bf16[32,1152]{1,0:T(8,128)(2,1)}) custom-call(s32[2]{0:T(128)} %pad_add_fusion.info, f32[32,2048]{1,0:T(8,128)} %dynamic-slice_bitcast_fusion.2.keep, bf16[32,2048]{1,0:T(8,128)(2,1)} %copy-done.3, bf16[32,2048]{1,0:T(8,128)(2,1)} %bitcast.67), custom_call_target="tpu_custom_call" | custom-call | flops 262144 | bytes 1048576 | tf_op jit(solution)/shard_map/out_grad/pallas_call | solution.py:273
  43.6 0.9 constant_dynamic-update-slice_fusion.1
  44.5 0.6 collective-permute-done.6
  45.1 3.6 %collective-permute-start.7 = (bf16[64,1152]{1,0:T(8,128)(2,1)S(1)}, bf16[64,1152]{1,0:T(8,128)(2,1)S(1)}, u32[]{:S(2)}, u32[]{:S(2)}) collective-permute-start(bf16[64,1152]{1,0:T(8,128)(2,1)S(1)} %get-tuple-element.95), channel_id=1, source_target_pairs={{2,0},{4,2},{6,4},{0,6},{3,1},{5,3},{7,5},{1,7},{10,8},{12,10},{14... | collective-permute-start | bytes 442376 | tf_op jit(solution)/shard_map/ppermute | solution.py:213
  48.7 1.1 collective-permute-start.8
  49.8 3.1 %collective-permute-done.7 = bf16[64,1152]{1,0:T(8,128)(2,1)S(1)} collective-permute-done((bf16[64,1152]{1,0:T(8,128)(2,1)S(1)}, bf16[64,1152]{1,0:T(8,128)(2,1)S(1)}, u32[]{:S(2)}, u32[]{:S(2)}) %collective-permute-start.7) | collective-permute-done | bytes 147488 | tf_op jit(solution)/shard_map/ppermute | solution.py:213
  53.0 8.7 %collective-permute-done.8 = bf16[64,1152]{1,0:T(8,128)(2,1)S(1)} collective-permute-done((bf16[64,1152]{1,0:T(8,128)(2,1)S(1)}, bf16[64,1152]{1,0:T(8,128)(2,1)S(1)}, u32[]{:S(2)}, u32[]{:S(2)}) %collective-permute-start.8) | collective-permute-done | bytes 147488 | tf_op jit(solution)/shard_map/ppermute | solution.py:213
  61.8 1.3 collective-permute-start.10
  63.1 1.3 collective-permute-start.12
  64.4 14.0 %collective-permute-done.10.refs_6_.refs_7_ = bf16[256,1152]{1,0:T(8,128)(2,1)S(1)} collective-permute-done((bf16[256,1152]{1,0:T(8,128)(2,1)S(1)}, bf16[256,1152]{1,0:T(8,128)(2,1)S(1)}, u32[]{:S(2)}, u32[]{:S(2)}) %collective-permute-start.10) | collective-permute-done | bytes 589856 | tf_op jit(solution)/shard_map/ppermute | solution.py:288
  78.4 1.5 collective-permute-start.11
  79.9 1.7 %collective-permute-done.12.refs_10_.refs_11_ = bf16[256,1152]{1,0:T(8,128)(2,1)} collective-permute-done((bf16[256,1152]{1,0:T(8,128)(2,1)S(1)}, bf16[256,1152]{1,0:T(8,128)(2,1)}, u32[]{:S(2)}, u32[]{:S(2)}) %collective-permute-start.12) | collective-permute-done | bytes 589856 | tf_op jit(solution)/shard_map/ppermute | solution.py:289
  81.6 1.3 copy-done
  83.0 15.6 %attention_backward_1_3.1 = (f32[1024,1024]{1,0:T(8,128)}, f32[1024,1024]{1,0:T(8,128)}, bf16[256,1024]{1,0:T(8,128)(2,1)}, bf16[256,1024]{1,0:T(8,128)(2,1)}) custom-call(s32[2]{0:T(128)} %pad_add_fusion.info, bf16[512,2048]{1,0:T(8,128)(2,1)} %bitcast.56, bf16[512,1024]{1,0:T(8,128)(2,1)} %collective-permute-done.4.refs_1_, bf16[512,2048]{1,0:T(8,128)(2,1)} %bitcast.59, ...), custom_call_target="tpu_custom_call" | custom-call | flops 10737418240 | bytes 16777216 | tf_op jit(solution)/shard_map/attention_backward_1_3/pallas_call | solution.py:183
  98.5 2.9 %collective-permute-start.13 = (bf16[256,1024]{1,0:T(8,128)(2,1)}, bf16[256,1024]{1,0:T(8,128)(2,1)S(1)}, u32[]{:S(2)}, u32[]{:S(2)}) collective-permute-start(bf16[256,1024]{1,0:T(8,128)(2,1)} %get-tuple-element.48), channel_id=1, source_target_pairs={{0,8},{8,16},{16,24},{1,9},{9,17},{17,25},{2,10},{10,18},{18,26},{... | collective-permute-start | bytes 1572872 | tf_op jit(solution)/shard_map/ppermute | solution.py:295
  101.4 1.3 collective-permute-start.14
  102.7 12.3 %attention_backward_2.1 = (f32[1024,1024]{1,0:T(8,128)}, f32[1024,1024]{1,0:T(8,128)}, bf16[256,1024]{1,0:T(8,128)(2,1)}) custom-call(s32[2]{0:T(128)} %pad_add_fusion.info, bf16[512,2048]{1,0:T(8,128)(2,1)} %bitcast.57, bf16[512,1024]{1,0:T(8,128)(2,1)} %collective-permute-done.4.refs_1_, ...), custom_call_target="tpu_custom_call", output_to_operand_aliasing={{0}: (9, {}), {1}: (10, {})} | custom-call | flops 5368709120 | bytes 16777216 | tf_op jit(solution)/shard_map/attention_backward_2/pallas_call | solution.py:183
  115.0 1.1 fusion.8
  116.2 2.5 %collective-permute-start.17 = (bf16[64,1024]{1,0:T(8,128)(2,1)S(1)}, bf16[64,1024]{1,0:T(8,128)(2,1)S(1)}, u32[]{:S(2)}, u32[]{:S(2)}) collective-permute-start(bf16[64,1024]{1,0:T(8,128)(2,1)S(1)} %get-tuple-element.86), channel_id=1, source_target_pairs={{2,0},{4,2},{6,4},{0,6},{3,1},{5,3},{7,5},{1,7},{10,8},{12,10},{14... | collective-permute-start | bytes 393224 | tf_op jit(solution)/shard_map/ppermute | solution.py:213
  118.7 0.7 collective-permute-start.15
  119.3 11.4 %attention_backward_0.1 = (bf16[512,1024]{1,0:T(8,128)(2,1)}, bf16[512,1024]{1,0:T(8,128)(2,1)}, bf16[512,1024]{1,0:T(8,128)(2,1)}, bf16[512,1024]{1,0:T(8,128)(2,1)}, bf16[256,1024]{1,0:T(8,128)(2,1)}) custom-call(s32[2]{0:T(128)} %pad_add_fusion.info, bf16[512,2048]{1,0:T(8,128)(2,1)} %bitcast.58, bf16[512,1024]{1,0:T(8,128)(2,1)} %collective-permute-done.4.refs_1_, ...), custom_call_target="tpu_custom_call" | custom-call | flops 5368709120 | bytes 16777216 | tf_op jit(solution)/shard_map/attention_backward_0/pallas_call | solution.py:183
  130.9 0.5 collective-permute-start.23
  131.4 3.9 %collective-permute-start.21 = (bf16[64,1024]{1,0:T(8,128)(2,1)S(1)}, bf16[64,1024]{1,0:T(8,128)(2,1)S(1)}, u32[]{:S(2)}, u32[]{:S(2)}) collective-permute-start(bf16[64,1024]{1,0:T(8,128)(2,1)S(1)} %add_convert_fusion.2), channel_id=1, source_target_pairs={{0,16},{8,24},{1,17},{9,25},{2,18},{10,26},{3,19},{11,27},{4,20},{... | collective-permute-start | bytes 393224 | tf_op jit(solution)/shard_map/ppermute | solution.py:311
  135.3 1.3 add_convert_fusion
  136.7 2.0 %collective-permute-start.20 = (bf16[64,1024]{1,0:T(8,128)(2,1)S(1)}, bf16[64,1024]{1,0:T(8,128)(2,1)S(1)}, u32[]{:S(2)}, u32[]{:S(2)}) collective-permute-start(bf16[64,1024]{1,0:T(8,128)(2,1)S(1)} %get-tuple-element.82), channel_id=1, source_target_pairs={{2,0},{4,2},{6,4},{0,6},{3,1},{5,3},{7,5},{1,7},{10,8},{12,10},{14... | collective-permute-start | bytes 393224 | tf_op jit(solution)/shard_map/ppermute | solution.py:213
  138.6 1.0 collective-permute-start.19
  139.7 0.3 broadcast_select_fusion.1
  139.9 1.5 maximum_bitcast_fusion.1
  141.4 1.5 maximum_bitcast_fusion
  143.0 8.3 %collective-permute-done.19 = bf16[64,1024]{1,0:T(8,128)(2,1)S(1)} collective-permute-done((bf16[64,1024]{1,0:T(8,128)(2,1)S(1)}, bf16[64,1024]{1,0:T(8,128)(2,1)S(1)}, u32[]{:S(2)}, u32[]{:S(2)}) %collective-permute-start.19) | collective-permute-done | bytes 131104 | tf_op jit(solution)/shard_map/ppermute | solution.py:213
  151.5 1.2 collective-permute-done.24
  152.7 0.7 maximum_bitcast_fusion.2
  (55 shorter events, 0.8 us)
Async XLA Ops:
  2.4 31.6 %all-to-all-start = ((bf16[8,32,1024]{2,1,0:T(8,128)(2,1)}), bf16[8,32,1024]{2,1,0:T(8,128)(2,1)S(1)}, u32[]{:S(2)}, u32[]{:S(2)}) async-start(bf16[8,32,1024]{2,1,0:T(8,128)(2,1)} %spread.1), calls=%async_computation | async-start | bytes 1048576 | tf_op jit(solution)/shard_map/all_to_all | solution.py:209
  10.5 13.4 %collective-permute-start = (bf16[2,32,2048]{2,1,0:T(8,128)(2,1)}, bf16[2,32,2048]{2,1,0:T(8,128)(2,1)}, u32[]{:S(2)}, u32[]{:S(2)}) collective-permute-start(bf16[2,32,2048]{2,1,0:T(8,128)(2,1)} %get-tuple-element.79), channel_id=1, source_target_pairs={{96,0},{0,32},{32,64},{64,96},{97,1},{1,33},{33,65},{65,97},{98,2}... | collective-permute-start | bytes 786440 | tf_op jit(solution)/shard_map/ppermute | solution.py:213
  12.0 11.9 %collective-permute-start.1 = (bf16[2,32,2048]{2,1,0:T(8,128)(2,1)}, bf16[2,32,2048]{2,1,0:T(8,128)(2,1)}, u32[]{:S(2)}, u32[]{:S(2)}) collective-permute-start(bf16[2,32,2048]{2,1,0:T(8,128)(2,1)} %get-tuple-element.80), channel_id=1, source_target_pairs={{64,0},{96,32},{0,64},{32,96},{65,1},{97,33},{1,65},{33,97},{66,2}... | collective-permute-start | bytes 786440 | tf_op jit(solution)/shard_map/ppermute | solution.py:213
  13.1 13.9 %collective-permute-start.2 = (bf16[2,32,2048]{2,1,0:T(8,128)(2,1)S(1)}, bf16[2,32,2048]{2,1,0:T(8,128)(2,1)}, u32[]{:S(2)}, u32[]{:S(2)}) collective-permute-start(bf16[2,32,2048]{2,1,0:T(8,128)(2,1)S(1)} %get-tuple-element.81), channel_id=1, source_target_pairs={{32,0},{64,32},{96,64},{0,96},{33,1},{65,33},{97,65},{1,97},{34,2}... | collective-permute-start | bytes 786440 | tf_op jit(solution)/shard_map/ppermute | solution.py:213
  15.3 4.7 %copy-start.7 = (s32[1,8]{1,0:T(1,128)S(1)}, s32[1,8]{1,0:T(1,128)}, u32[]{:S(2)}) copy-start(s32[1,8]{1,0:T(1,128)} %param.12) | copy-start | bytes 100
  15.3 5.5 %copy-start.4 = (f32[1,1024,16]{1,2,0:T(8,128)S(1)}, f32[1,1024,16]{1,2,0:T(8,128)}, u32[]{:S(2)}) copy-start(f32[1,1024,16]{1,2,0:T(8,128)} %param.11) | copy-start | bytes 196612
  16.6 23.7 %collective-permute-start.5 = (bf16[512,1024]{1,0:T(8,128)(2,1)S(1)}, bf16[512,1024]{1,0:T(8,128)(2,1)}, u32[]{:S(2)}, u32[]{:S(2)}) collective-permute-start(bf16[512,1024]{1,0:T(8,128)(2,1)S(1)} %dynamic-slice_bitcast_fusion), channel_id=1, source_target_pairs={{0,1},{1,0},{2,3},{3,2},{4,5},{5,4},{6,7},{7,6},{8,9},{9,8},{10,11... | collective-permute-start | bytes 3145736 | tf_op jit(solution)/shard_map/ppermute | solution.py:205
  19.0 21.4 %collective-permute-start.4 = (bf16[512,1024]{1,0:T(8,128)(2,1)}, bf16[512,1024]{1,0:T(8,128)(2,1)}, u32[]{:S(2)}, u32[]{:S(2)}) collective-permute-start(bf16[512,1024]{1,0:T(8,128)(2,1)} %dynamic-slice_bitcast_fusion.1), channel_id=1, source_target_pairs={{0,1},{1,0},{2,3},{3,2},{4,5},{5,4},{6,7},{7,6},{8,9},{9,8},{10,11... | collective-permute-start | bytes 3145736 | tf_op jit(solution)/shard_map/ppermute | solution.py:205
  28.4 11.9 %collective-permute-start.3 = (bf16[32,2048]{1,0:T(8,128)(2,1)S(1)}, bf16[32,2048]{1,0:T(8,128)(2,1)S(1)}, u32[]{:S(2)}, u32[]{:S(2)}) collective-permute-start(bf16[32,2048]{1,0:T(8,128)(2,1)S(1)} %fusion.6), channel_id=1, source_target_pairs={{0,128},{128,0},{1,129},{129,1},{2,130},{130,2},{3,131},{131,3},{4... | collective-permute-start | bytes 393224 | tf_op jit(solution)/shard_map/ppermute | solution.py:205
  35.9 45.8 %all-to-all-start.1 = ((bf16[4,256,1024]{2,1,0:T(8,128)(2,1)}), bf16[4,256,1024]{2,1,0:T(8,128)(2,1)S(1)}, u32[]{:S(2)}, u32[]{:S(2)}) async-start(bf16[4,256,1024]{2,1,0:T(8,128)(2,1)} %broadcast_in_dim.44), calls=%async_computation.1 | async-start | bytes 4194304 | tf_op jit(solution)/shard_map/all_to_all | solution.py:209
  40.3 0.7 copy-start.3
  43.6 1.5 collective-permute-start.6
  45.1 7.8 %collective-permute-start.7 = (bf16[64,1152]{1,0:T(8,128)(2,1)S(1)}, bf16[64,1152]{1,0:T(8,128)(2,1)S(1)}, u32[]{:S(2)}, u32[]{:S(2)}) collective-permute-start(bf16[64,1152]{1,0:T(8,128)(2,1)S(1)} %get-tuple-element.95), channel_id=1, source_target_pairs={{2,0},{4,2},{6,4},{0,6},{3,1},{5,3},{7,5},{1,7},{10,8},{12,10},{14... | collective-permute-start | bytes 442376 | tf_op jit(solution)/shard_map/ppermute | solution.py:213
  48.7 13.0 %collective-permute-start.9 = (bf16[64,1152]{1,0:T(8,128)(2,1)S(1)}, bf16[64,1152]{1,0:T(8,128)(2,1)S(1)}, u32[]{:S(2)}, u32[]{:S(2)}) collective-permute-start(bf16[64,1152]{1,0:T(8,128)(2,1)S(1)} %get-tuple-element.95), channel_id=1, source_target_pairs={{6,0},{0,2},{2,4},{4,6},{7,1},{1,3},{3,5},{5,7},{14,8},{8,10},{10,... | collective-permute-start | bytes 442376 | tf_op jit(solution)/shard_map/ppermute | solution.py:213
  48.7 13.0 %collective-permute-start.8 = (bf16[64,1152]{1,0:T(8,128)(2,1)S(1)}, bf16[64,1152]{1,0:T(8,128)(2,1)S(1)}, u32[]{:S(2)}, u32[]{:S(2)}) collective-permute-start(bf16[64,1152]{1,0:T(8,128)(2,1)S(1)} %get-tuple-element.95), channel_id=1, source_target_pairs={{4,0},{6,2},{0,4},{2,6},{5,1},{7,3},{1,5},{3,7},{12,8},{14,10},{8,... | collective-permute-start | bytes 442376 | tf_op jit(solution)/shard_map/ppermute | solution.py:213
  61.8 36.7 %copy-start.5 = (bf16[256,1152]{1,0:T(8,128)(2,1)}, bf16[256,1152]{1,0:T(8,128)(2,1)S(1)}, u32[]{:S(2)}) copy-start(bf16[256,1152]{1,0:T(8,128)(2,1)S(1)} %constant_dynamic-update-slice_fusion.2.refs_6_.refs_7_) | copy-start | bytes 1769476
  61.8 16.6 %collective-permute-start.10 = (bf16[256,1152]{1,0:T(8,128)(2,1)S(1)}, bf16[256,1152]{1,0:T(8,128)(2,1)S(1)}, u32[]{:S(2)}, u32[]{:S(2)}) collective-permute-start(bf16[256,1152]{1,0:T(8,128)(2,1)S(1)} %constant_dynamic-update-slice_fusion.2.refs_6_.refs_7_), channel_id=1, source_target_pairs={{8,0},{16,8},{24,16},{9,1},{17,9},{25,17},{10,2},{18,10},{26,18},{... | collective-permute-start | bytes 1769480 | tf_op jit(solution)/shard_map/ppermute | solution.py:288
  63.1 18.6 %collective-permute-start.12 = (bf16[256,1152]{1,0:T(8,128)(2,1)S(1)}, bf16[256,1152]{1,0:T(8,128)(2,1)}, u32[]{:S(2)}, u32[]{:S(2)}) collective-permute-start(bf16[256,1152]{1,0:T(8,128)(2,1)S(1)} %constant_dynamic-update-slice_fusion.2.refs_6_.refs_7_), channel_id=1, source_target_pairs={{24,0},{25,1},{26,2},{27,3},{28,4},{29,5},{30,6},{31,7},{56,32},{5... | collective-permute-start | bytes 1769480 | tf_op jit(solution)/shard_map/ppermute | solution.py:289
  78.4 3.2 %copy-start.6 = (bf16[256,1152]{1,0:T(8,128)(2,1)}, bf16[256,1152]{1,0:T(8,128)(2,1)S(1)}, u32[]{:S(2)}) copy-start(bf16[256,1152]{1,0:T(8,128)(2,1)S(1)} %collective-permute-done.10.refs_6_.refs_7_) | copy-start | bytes 1769476
  78.4 24.3 %collective-permute-start.11 = (bf16[256,1152]{1,0:T(8,128)(2,1)S(1)}, bf16[256,1152]{1,0:T(8,128)(2,1)}, u32[]{:S(2)}, u32[]{:S(2)}) collective-permute-start(bf16[256,1152]{1,0:T(8,128)(2,1)S(1)} %collective-permute-done.10.refs_6_.refs_7_), channel_id=1, source_target_pairs={{8,0},{16,8},{9,1},{17,9},{10,2},{18,10},{11,3},{19,11},{12,4},{20... | collective-permute-start | bytes 1769480 | tf_op jit(solution)/shard_map/ppermute | solution.py:291
  81.6 1.3 copy-start
  98.5 16.5 %collective-permute-start.13 = (bf16[256,1024]{1,0:T(8,128)(2,1)}, bf16[256,1024]{1,0:T(8,128)(2,1)S(1)}, u32[]{:S(2)}, u32[]{:S(2)}) collective-permute-start(bf16[256,1024]{1,0:T(8,128)(2,1)} %get-tuple-element.48), channel_id=1, source_target_pairs={{0,8},{8,16},{16,24},{1,9},{9,17},{17,25},{2,10},{10,18},{18,26},{... | collective-permute-start | bytes 1572872 | tf_op jit(solution)/shard_map/ppermute | solution.py:295
  101.4 13.6 %collective-permute-start.14 = (bf16[256,1024]{1,0:T(8,128)(2,1)}, bf16[256,1024]{1,0:T(8,128)(2,1)S(1)}, u32[]{:S(2)}, u32[]{:S(2)}) collective-permute-start(bf16[256,1024]{1,0:T(8,128)(2,1)} %get-tuple-element.49), channel_id=1, source_target_pairs={{0,24},{1,25},{2,26},{3,27},{4,28},{5,29},{6,30},{7,31},{32,56},{3... | collective-permute-start | bytes 1572872 | tf_op jit(solution)/shard_map/ppermute | solution.py:296
  116.2 14.6 %collective-permute-start.17 = (bf16[64,1024]{1,0:T(8,128)(2,1)S(1)}, bf16[64,1024]{1,0:T(8,128)(2,1)S(1)}, u32[]{:S(2)}, u32[]{:S(2)}) collective-permute-start(bf16[64,1024]{1,0:T(8,128)(2,1)S(1)} %get-tuple-element.86), channel_id=1, source_target_pairs={{2,0},{4,2},{6,4},{0,6},{3,1},{5,3},{7,5},{1,7},{10,8},{12,10},{14... | collective-permute-start | bytes 393224 | tf_op jit(solution)/shard_map/ppermute | solution.py:213
  118.7 12.1 %collective-permute-start.16 = (bf16[64,1024]{1,0:T(8,128)(2,1)S(1)}, bf16[64,1024]{1,0:T(8,128)(2,1)S(1)}, u32[]{:S(2)}, u32[]{:S(2)}) collective-permute-start(bf16[64,1024]{1,0:T(8,128)(2,1)S(1)} %get-tuple-element.87), channel_id=1, source_target_pairs={{4,0},{6,2},{0,4},{2,6},{5,1},{7,3},{1,5},{3,7},{12,8},{14,10},{8,... | collective-permute-start | bytes 393224 | tf_op jit(solution)/shard_map/ppermute | solution.py:213
  118.7 12.1 %collective-permute-start.15 = (bf16[64,1024]{1,0:T(8,128)(2,1)S(1)}, bf16[64,1024]{1,0:T(8,128)(2,1)S(1)}, u32[]{:S(2)}, u32[]{:S(2)}) collective-permute-start(bf16[64,1024]{1,0:T(8,128)(2,1)S(1)} %get-tuple-element.88), channel_id=1, source_target_pairs={{6,0},{0,2},{2,4},{4,6},{7,1},{1,3},{3,5},{5,7},{14,8},{8,10},{10,... | collective-permute-start | bytes 393224 | tf_op jit(solution)/shard_map/ppermute | solution.py:213
  130.7 8.9 %copy-start.1 = (bf16[512,1024]{1,0:T(8,128)(2,1)S(1)}, bf16[512,1024]{1,0:T(8,128)(2,1)}, u32[]{:S(2)}) copy-start(bf16[512,1024]{1,0:T(8,128)(2,1)} %get-tuple-element.64) | copy-start | bytes 3145732
  130.7 8.9 %copy-start.2 = (bf16[512,1024]{1,0:T(8,128)(2,1)S(1)}, bf16[512,1024]{1,0:T(8,128)(2,1)}, u32[]{:S(2)}) copy-start(bf16[512,1024]{1,0:T(8,128)(2,1)} %get-tuple-element.66) | copy-start | bytes 3145732
  130.8 8.9 %collective-permute-start.22 = (bf16[512,1024]{1,0:T(8,128)(2,1)}, bf16[512,1024]{1,0:T(8,128)(2,1)S(1)}, u32[]{:S(2)}, u32[]{:S(2)}) collective-permute-start(bf16[512,1024]{1,0:T(8,128)(2,1)} %get-tuple-element.65), channel_id=1, source_target_pairs={{0,1},{1,0},{2,3},{3,2},{4,5},{5,4},{6,7},{7,6},{8,9},{9,8},{10,11... | collective-permute-start | bytes 3145736 | tf_op jit(solution)/shard_map/ppermute | solution.py:205
  130.9 8.8 %collective-permute-start.23 = (bf16[512,1024]{1,0:T(8,128)(2,1)}, bf16[512,1024]{1,0:T(8,128)(2,1)S(1)}, u32[]{:S(2)}, u32[]{:S(2)}) collective-permute-start(bf16[512,1024]{1,0:T(8,128)(2,1)} %get-tuple-element.67), channel_id=1, source_target_pairs={{0,1},{1,0},{2,3},{3,2},{4,5},{5,4},{6,7},{7,6},{8,9},{9,8},{10,11... | collective-permute-start | bytes 3145736 | tf_op jit(solution)/shard_map/ppermute | solution.py:205
  131.4 11.5 %collective-permute-start.21 = (bf16[64,1024]{1,0:T(8,128)(2,1)S(1)}, bf16[64,1024]{1,0:T(8,128)(2,1)S(1)}, u32[]{:S(2)}, u32[]{:S(2)}) collective-permute-start(bf16[64,1024]{1,0:T(8,128)(2,1)S(1)} %add_convert_fusion.2), channel_id=1, source_target_pairs={{0,16},{8,24},{1,17},{9,25},{2,18},{10,26},{3,19},{11,27},{4,20},{... | collective-permute-start | bytes 393224 | tf_op jit(solution)/shard_map/ppermute | solution.py:311
  136.7 6.3 %collective-permute-start.20 = (bf16[64,1024]{1,0:T(8,128)(2,1)S(1)}, bf16[64,1024]{1,0:T(8,128)(2,1)S(1)}, u32[]{:S(2)}, u32[]{:S(2)}) collective-permute-start(bf16[64,1024]{1,0:T(8,128)(2,1)S(1)} %get-tuple-element.82), channel_id=1, source_target_pairs={{2,0},{4,2},{6,4},{0,6},{3,1},{5,3},{7,5},{1,7},{10,8},{12,10},{14... | collective-permute-start | bytes 393224 | tf_op jit(solution)/shard_map/ppermute | solution.py:213
  138.6 12.6 %collective-permute-start.19 = (bf16[64,1024]{1,0:T(8,128)(2,1)S(1)}, bf16[64,1024]{1,0:T(8,128)(2,1)S(1)}, u32[]{:S(2)}, u32[]{:S(2)}) collective-permute-start(bf16[64,1024]{1,0:T(8,128)(2,1)S(1)} %get-tuple-element.83), channel_id=1, source_target_pairs={{4,0},{6,2},{0,4},{2,6},{5,1},{7,3},{1,5},{3,7},{12,8},{14,10},{8,... | collective-permute-start | bytes 393224 | tf_op jit(solution)/shard_map/ppermute | solution.py:213
  139.6 11.6 %collective-permute-start.18 = (bf16[64,1024]{1,0:T(8,128)(2,1)S(1)}, bf16[64,1024]{1,0:T(8,128)(2,1)S(1)}, u32[]{:S(2)}, u32[]{:S(2)}) collective-permute-start(bf16[64,1024]{1,0:T(8,128)(2,1)S(1)} %get-tuple-element.84), channel_id=1, source_target_pairs={{6,0},{0,2},{2,4},{4,6},{7,1},{1,3},{3,5},{5,7},{14,8},{8,10},{10,... | collective-permute-start | bytes 393224 | tf_op jit(solution)/shard_map/ppermute | solution.py:213
  151.4 1.3 collective-permute-start.24
